TPU v7x, 256 devices: a whole 4x4x8 slice. The times are simulated.
256 devices in a mesh: phase: 4 (over x), ctx: 64 (over z, y, core).
Axes of the slice: x: 4, y: 4, z: 8, core: 2. Of those that a mesh axis runs over, the one named last changes fastest.
Arguments:
- hidden: bfloat16 [4, 8192, 4096], P('phase', 'ctx'), may hold values from -6 to 6
- queries: bfloat16 [4, 8192, 2048], P('phase', 'ctx'), may hold values from -400 to 400
- key_value_weight: bfloat16 [4, 4096, 1024], P('phase'), may hold values from -0.09375 to 0.09375
- doc_ids: int32 [4, 8192], P('phase'), may hold values from 0 to 7, never falling along the last dimension, each value on 1 to 6144 neighbouring positions
- scored: int32 [4, 8192], P('phase', 'ctx'), may hold values 0 or 1
Outputs:
- passed: bfloat16 [4, 8192, 2048], P('phase', 'ctx')
Inputs may be any that keep to these rules, and one draw needn't show every extreme that they name: doc_ids never fall along a sequence; one document spans exactly 6144 tokens.
All inputs are finite; a program needn't handle non-finite values. No bound on the sum of `scored` on one device may be relied on, other than what follows from the above.
Results may differ from a plain program's by a relative error of at most 0.008.
The roundings to bfloat16 on the way count: a program that leaves them out, or rounds other values in their place, can miss the bound.
Values may be sent and summed in bfloat16 or wider, within the bound.
A program may use at most 128 MiB of HBM per device.

v0:
```python
import math
import jax
import jax.numpy as jnp
from jax import lax
from jax.sharding import PartitionSpec as P

QUERY_HEADS = 16
KEY_VALUE_HEADS = 4
HEAD_SIZE = 128
rope_base = 500000.0


def from_behind(block, axis, distance):
    devices = range(lax.axis_size(axis))
    route = [((i - distance) % len(devices), i) for i in devices]
    return lax.ppermute(block, axis, route)


def apply_rotary(key_heads, token_positions):
    half_dim = key_heads.shape[-1] // 2
    frequency = rope_base ** (-jnp.arange(half_dim, dtype=jnp.float32) * 2.0 / key_heads.shape[-1])
    angles = token_positions.astype(jnp.float32)[:, None] * frequency[None, :]
    cosine_part = jnp.cos(angles)[:, None, :]
    sine_part = jnp.sin(angles)[:, None, :]
    lower_half = key_heads[..., :half_dim]
    upper_half = key_heads[..., half_dim:]
    return jnp.concatenate(
        [
            lower_half * cosine_part - upper_half * sine_part,
            upper_half * cosine_part + lower_half * sine_part,
        ],
        axis=-1,
    )


def per_device(hidden, queries, key_value_weight, doc_ids, scored):
    count_of_rows = hidden.shape[1]
    first_row = lax.axis_index("ctx") * count_of_rows
    token_positions = first_row + jnp.arange(count_of_rows, dtype=jnp.int32)
    wide = hidden[0].astype(jnp.float32)
    normed = (wide * lax.rsqrt(jnp.mean(wide * wide, axis=-1, keepdims=True) + 1e-05)).astype(
        jnp.bfloat16
    )
    projected_rows = jnp.dot(normed, key_value_weight[0], preferred_element_type=jnp.float32)
    key_value_width = KEY_VALUE_HEADS * HEAD_SIZE
    key_matrix = (
        apply_rotary(
            projected_rows[:, :key_value_width].reshape(count_of_rows, KEY_VALUE_HEADS, HEAD_SIZE),
            token_positions,
        )
        .astype(jnp.bfloat16)
        .reshape(count_of_rows, key_value_width)
    )
    value_matrix = projected_rows[:, key_value_width:].astype(jnp.bfloat16)
    query_group_width = QUERY_HEADS // KEY_VALUE_HEADS
    query_head_count = queries[0].reshape(
        count_of_rows, KEY_VALUE_HEADS, query_group_width, HEAD_SIZE
    )
    sequence_docs = doc_ids[0]
    own_docs = lax.dynamic_slice_in_dim(sequence_docs, first_row, count_of_rows, 0)
    score_scale = 1.0 / math.sqrt(HEAD_SIZE)
    stacked = jnp.concatenate([key_matrix, value_matrix], axis=1)
    collected_rows = lax.all_gather(stacked, "ctx", axis=0, tiled=True)
    sequence_length = collected_rows.shape[0]
    every_key_row = collected_rows[:, :key_value_width].reshape(
        sequence_length, KEY_VALUE_HEADS, HEAD_SIZE
    )
    every_value_row = collected_rows[:, key_value_width:].reshape(
        sequence_length, KEY_VALUE_HEADS, HEAD_SIZE
    )
    head_outputs = []
    for key_value_head in range(KEY_VALUE_HEADS):
        key_part = every_key_row[:, key_value_head : key_value_head + 1]
        key_count = key_part.shape[0]
        scores = (
            jnp.einsum(
                "qhgd,khd->hgqk",
                query_head_count[:, key_value_head : key_value_head + 1],
                key_part,
                preferred_element_type=jnp.float32,
            )
            * score_scale
        )
        key_pos = jnp.arange(key_count, dtype=jnp.int32)
        allowed = (key_pos[None, :] <= token_positions[:, None]) & (
            sequence_docs[None, :] == own_docs[:, None]
        )
        scores = jnp.where(allowed[None, None], scores, jnp.float32(-1e30))
        row_max = jnp.max(scores, axis=-1, keepdims=True)
        expo = jnp.exp(scores - row_max)
        total = jnp.sum(expo, axis=-1)
        weights = expo.astype(jnp.bfloat16)
        summed = jnp.einsum(
            "hgqk,khd->hgqd",
            weights,
            every_value_row[:, key_value_head : key_value_head + 1],
            preferred_element_type=jnp.float32,
        )
        head_outputs.append(summed / total[..., None])
    attended = jnp.transpose(jnp.concatenate(head_outputs, axis=0), (2, 0, 1, 3))
    flat = (
        attended.reshape(count_of_rows, QUERY_HEADS * HEAD_SIZE)
        * scored[0].astype(jnp.float32)[:, None]
    )
    outgoing = flat.astype(jnp.bfloat16)[None]
    return from_behind(outgoing, "phase", 1)


def solution(mesh):
    placed = (
        P("phase", "ctx", None),
        P("phase", "ctx", None),
        P("phase", None, None),
        P("phase", None),
        P("phase", "ctx"),
    )
    return jax.shard_map(
        per_device, mesh=mesh, in_specs=placed, out_specs=P("phase", "ctx", None), check_vma=False
    )
```

profile of v0, /device:TPU:1, one launch (start us, length us, event | category | flops | bytes accessed | tf_op | source)
XLA Modules:
  0.0 297.0 jit_solution(15836771491093661803)
XLA Ops:
  6.5 0.0 all-gather.2.cloned.1.call-start
  6.5 1.5 fusion.27
  8.1 0.0 copy-start.1
  8.1 0.0 copy-start.2
  8.1 0.0 copy-start.3
  8.1 5.1 %fusion.20 = f32[128,1024]{1,0:T(8,128)S(1)} fusion(bf16[1,4096,1024]{2,1,0:T(8,128)(2,1)} %param.7, bf16[1,128,4096]{2,1,0:T(8,128)(2,1)} %param.5, f32[128]{0:T(128)S(1)} %add_rsqrt_fusion), kind=kOutput, calls=%fused_computation.24 | convolution fusion | flops 1075314688 | bytes 9961984 | tf_op jit(solution)/shard_map/dot_general | solution.py:44
  13.2 0.1 reshape.293
  13.3 0.3 multiply_cosine_fusion
  13.7 0.3 subtract_convert_fusion
  13.9 0.2 pad_maximum_fusion.2
  14.2 0.7 pad_maximum_fusion.1
  14.9 0.0 all-gather.2.cloned.1.call-update
  14.9 0.0 copy-done.1
  14.9 0.3 copy.20
  15.2 0.0 copy-done.2
  15.2 0.0 copy-done.3
  15.3 3.9 %fusion.26 = pred[128,8192]{0,1:T(8,128)(4,1)S(1)} fusion(s32[128]{0:T(128)S(1)} %dynamic-slice_bitcast_fusion, s32[128]{0:T(128)S(1)} %get-tuple-element.23, s32[8192]{0:T(1024)S(1)} %bitcast.163), kind=kLoop, calls=%fused_computation.31 | loop fusion | flops 3145728 | bytes 1082368 | tf_op jit(solution)/shard_map/and | solution.py:85
  19.2 100.0 %all-gather.2.cloned.1.call-done = bf16[8192,1024]{1,0:T(8,128)(2,1)} async-done(((bf16[128,1024]{1,0:T(8,128)(2,1)}), bf16[8192,1024]{1,0:T(8,128)(2,1)}) %all-gather.2.cloned.1.call-update) | async-done | bytes 16777232 | tf_op jit(solution)/shard_map/all_gather | solution.py:63
  119.2 11.3 %fusion.57 = (bf16[8192,512]{1,0:T(8,128)(2,1)}, bf16[8192,512]{1,0:T(8,128)(2,1)}) fusion(bf16[8192,1024]{1,0:T(8,128)(2,1)} %all-gather.2.cloned.1.call-done), kind=kLoop, calls=%fused_computation.74 | loop fusion | bytes 33554432 | tf_op jit(solution)/shard_map/slice | solution.py:68
  130.5 11.3 %copy.41 = bf16[8192,512]{0,1:T(8,128)(2,1)} copy(bf16[8192,512]{1,0:T(8,128)(2,1)} %get-tuple-element.5) | data formatting | bytes 16777216 | tf_op jit(solution)/shard_map/reshape | solution.py:68
  141.9 12.5 %reshape.294 = bf16[8192,4,128]{2,1,0:T(4,128)(2,1)} reshape(bf16[8192,512]{1,0:T(8,128)(2,1)} %get-tuple-element.6) | data formatting | bytes 16777216 | tf_op jit(solution)/shard_map/reshape | solution.py:65
  154.4 26.4 %fusion.58 = (bf16[8192,1,128]{2,1,0:T(2,128)(2,1)S(1)}, bf16[8192,1,128]{2,1,0:T(2,128)(2,1)S(1)}, bf16[8192,1,128]{2,1,0:T(2,128)(2,1)}, bf16[8192,1,128]{2,1,0:T(2,128)(2,1)S(1)}) fusion(bf16[8192,4,128]{2,1,0:T(4,128)(2,1)} %reshape.294), kind=kLoop, calls=%fused_computation.75 | loop fusion | bytes 16777216 | tf_op jit(solution)/shard_map/slice | solution.py:73
  180.8 7.3 %fusion.62 = (f32[4,128]{1,0:T(4,128)S(1)}, f32[1,4,128,8192]{2,3,1,0:T(8,128)}) fusion(bf16[128,4,4,128]{0,3,2,1:T(8,128)(2,1)S(1)} %bitcast.158, bf16[8192,1,128]{2,1,0:T(2,128)(2,1)S(1)} %get-tuple-element.7, pred[128,8192]{0,1:T(8,128)(4,1)S(1)} %fusion.26), kind=kOutput, calls=%fused_computation.79 | convolution fusion | flops 1086324224 | bytes 22153216 | tf_op jit(solution)/shard_map/qhgd,khd->hgqk/dot_general | solution.py:76
  188.1 7.3 %fusion.60 = (f32[4,128]{1,0:T(4,128)S(1)}, f32[1,4,128,8192]{2,3,1,0:T(8,128)}) fusion(bf16[128,4,4,128]{0,3,2,1:T(8,128)(2,1)S(1)} %bitcast.159, bf16[8192,1,128]{2,1,0:T(2,128)(2,1)S(1)} %get-tuple-element.8, pred[128,8192]{0,1:T(8,128)(4,1)S(1)} %fusion.26), kind=kOutput, calls=%fused_computation.77 | convolution fusion | flops 1086324224 | bytes 22153216 | tf_op jit(solution)/shard_map/qhgd,khd->hgqk/dot_general | solution.py:76
  195.4 8.0 %fusion = f32[4,128]{1,0:T(4,128)S(1)} fusion(f32[1,4,128,8192]{2,3,1,0:T(8,128)} %get-tuple-element.22, f32[4,128]{1,0:T(4,128)S(1)} %get-tuple-element.21), kind=kLoop, calls=%fused_computation.8 | loop fusion | flops 8388096 | bytes 16781312 | tf_op jit(solution)/shard_map/reduce_sum | solution.py:91
  203.4 8.2 %fusion.32 = f32[1,4,128,128]{2,3,1,0:T(8,128)S(1)} fusion(f32[1,4,128,8192]{2,3,1,0:T(8,128)} %get-tuple-element.22, f32[4,128]{1,0:T(4,128)S(1)} %get-tuple-element.21, bf16[8192,4,128]{0,2,1:T(8,128)(2,1)} %bitcast.152, f32[4,128]{1,0:T(4,128)S(1)} %fusion), kind=kOutput, calls=%fused_computation.45 | convolution fusion | flops 1082195968 | bytes 19140608 | tf_op jit(solution)/shard_map/hgqk,khd->hgqd/dot_general | solution.py:93
  211.6 8.0 %fusion.4 = f32[4,128]{1,0:T(4,128)S(1)} fusion(f32[1,4,128,8192]{2,3,1,0:T(8,128)} %get-tuple-element.18, f32[4,128]{1,0:T(4,128)S(1)} %get-tuple-element.17), kind=kLoop, calls=%fused_computation.12 | loop fusion | flops 8388096 | bytes 16781312 | tf_op jit(solution)/shard_map/reduce_sum | solution.py:91
  219.5 0.0 copy-start
  219.5 8.1 %fusion.44 = f32[1,4,128,128]{2,3,1,0:T(8,128)S(1)} fusion(f32[1,4,128,8192]{2,3,1,0:T(8,128)} %get-tuple-element.18, f32[4,128]{1,0:T(4,128)S(1)} %get-tuple-element.17, bf16[8192,4,128]{0,2,1:T(8,128)(2,1)} %bitcast.153, f32[4,128]{1,0:T(4,128)S(1)} %fusion.4), kind=kOutput, calls=%fused_computation.49 | convolution fusion | flops 1082195968 | bytes 19140608 | tf_op jit(solution)/shard_map/hgqk,khd->hgqd/dot_general | solution.py:93
  227.7 0.0 copy-done
  227.7 7.3 %fusion.61 = (f32[4,128]{1,0:T(4,128)S(1)}, f32[1,4,128,8192]{2,3,1,0:T(8,128)}) fusion(bf16[128,4,4,128]{0,3,2,1:T(8,128)(2,1)S(1)} %bitcast.160, bf16[8192,1,128]{2,1,0:T(2,128)(2,1)S(1)} %copy-done, pred[128,8192]{0,1:T(8,128)(4,1)S(1)} %fusion.26), kind=kOutput, calls=%fused_computation.78 | convolution fusion | flops 1086324224 | bytes 22153216 | tf_op jit(solution)/shard_map/qhgd,khd->hgqk/dot_general | solution.py:76
  235.0 8.0 %fusion.2 = f32[4,128]{1,0:T(4,128)S(1)} fusion(f32[1,4,128,8192]{2,3,1,0:T(8,128)} %get-tuple-element.20, f32[4,128]{1,0:T(4,128)S(1)} %get-tuple-element.19), kind=kLoop, calls=%fused_computation.10 | loop fusion | flops 8388096 | bytes 16781312 | tf_op jit(solution)/shard_map/reduce_sum | solution.py:91
  243.0 8.0 %fusion.38 = f32[1,4,128,128]{2,3,1,0:T(8,128)S(1)} fusion(f32[1,4,128,8192]{2,3,1,0:T(8,128)} %get-tuple-element.20, f32[4,128]{1,0:T(4,128)S(1)} %get-tuple-element.19, bf16[8192,4,128]{0,2,1:T(8,128)(2,1)} %bitcast.154, f32[4,128]{1,0:T(4,128)S(1)} %fusion.2), kind=kOutput, calls=%fused_computation.47 | convolution fusion | flops 1082195968 | bytes 19140608 | tf_op jit(solution)/shard_map/hgqk,khd->hgqd/dot_general | solution.py:93
  250.9 7.3 %fusion.59 = (f32[4,128]{1,0:T(4,128)S(1)}, f32[1,4,128,8192]{2,3,1,0:T(8,128)}) fusion(bf16[128,4,4,128]{0,3,2,1:T(8,128)(2,1)S(1)} %bitcast.161, bf16[8192,1,128]{2,1,0:T(2,128)(2,1)S(1)} %get-tuple-element.10, pred[128,8192]{0,1:T(8,128)(4,1)S(1)} %fusion.26), kind=kOutput, calls=%fused_computation.76 | convolution fusion | flops 1086324224 | bytes 22153216 | tf_op jit(solution)/shard_map/qhgd,khd->hgqk/dot_general | solution.py:76
  258.3 8.0 %fusion.6 = f32[4,128]{1,0:T(4,128)S(1)} fusion(f32[1,4,128,8192]{2,3,1,0:T(8,128)} %get-tuple-element.16, f32[4,128]{1,0:T(4,128)S(1)} %get-tuple-element.15), kind=kLoop, calls=%fused_computation.14 | loop fusion | flops 8388096 | bytes 16781312 | tf_op jit(solution)/shard_map/reduce_sum | solution.py:91
  266.2 8.0 %fusion.50 = f32[1,4,128,128]{2,3,1,0:T(8,128)S(1)} fusion(f32[1,4,128,8192]{2,3,1,0:T(8,128)} %get-tuple-element.16, f32[4,128]{1,0:T(4,128)S(1)} %get-tuple-element.15, bf16[8192,4,128]{0,2,1:T(8,128)(2,1)} %bitcast.155, f32[4,128]{1,0:T(4,128)S(1)} %fusion.6), kind=kOutput, calls=%fused_computation.51 | convolution fusion | flops 1082195968 | bytes 19140608 | tf_op jit(solution)/shard_map/hgqk,khd->hgqd/dot_general | solution.py:93
  274.2 0.1 pad_maximum_fusion
  274.3 0.3 copy.36
  274.6 0.1 multiply_convert_fusion
  274.8 1.3 collective-permute-start
  276.0 13.3 %collective-permute-done = bf16[1,128,2048]{2,1,0:T(8,128)(2,1)S(1)} collective-permute-done((bf16[1,128,2048]{2,1,0:T(8,128)(2,1)S(1)}, bf16[1,128,2048]{2,1,0:T(8,128)(2,1)S(1)}, u32[]{:S(2)}, u32[]{:S(2)}) %collective-permute-start) | collective-permute-done | bytes 524320 | tf_op jit(solution)/shard_map/ppermute | solution.py:16
  289.3 0.8 copy.70
  (8 shorter events, 0.1 us)
Async XLA Ops:
  6.5 112.7 %all-gather.2.cloned.1.call-start = ((), (), s32[]{:S(2)}) async-start(), calls=%async_computation | async-start | bytes 17039360 | tf_op jit(solution)/shard_map/all_gather | solution.py:63
  8.1 6.8 %copy-start.1 = (bf16[1,128,2048]{2,1,0:T(8,128)(2,1)S(1)}, bf16[1,128,2048]{2,1,0:T(8,128)(2,1)}, u32[]{:S(2)}) copy-start(bf16[1,128,2048]{2,1,0:T(8,128)(2,1)} %param.6) | copy-start | bytes 1572868
  8.1 7.1 %copy-start.2 = (s32[1,8192]{1,0:T(1,128)S(1)}, s32[1,8192]{1,0:T(1,128)}, u32[]{:S(2)}) copy-start(s32[1,8192]{1,0:T(1,128)} %param.8) | copy-start | bytes 98308
  8.1 7.1 %copy-start.3 = (s32[1,128]{1,0:T(1,128)S(1)}, s32[1,128]{1,0:T(1,128)}, u32[]{:S(2)}) copy-start(s32[1,128]{1,0:T(1,128)} %param.9) | copy-start | bytes 1540
  219.5 8.1 %copy-start = (bf16[8192,1,128]{2,1,0:T(2,128)(2,1)S(1)}, bf16[8192,1,128]{2,1,0:T(2,128)(2,1)}, u32[]{:S(2)}) copy-start(bf16[8192,1,128]{2,1,0:T(2,128)(2,1)} %get-tuple-element.9) | copy-start | bytes 6291460
  274.8 14.6 %collective-permute-start = (bf16[1,128,2048]{2,1,0:T(8,128)(2,1)S(1)}, bf16[1,128,2048]{2,1,0:T(8,128)(2,1)S(1)}, u32[]{:S(2)}, u32[]{:S(2)}) collective-permute-start(bf16[1,128,2048]{2,1,0:T(8,128)(2,1)S(1)} %multiply_convert_fusion), channel_id=1, source_target_pairs={{192,0},{0,64},{64,128},{128,192},{193,1},{1,65},{65,129},{129,193... | collective-permute-start | bytes 1572872 | tf_op jit(solution)/shard_map/ppermute | solution.py:16
Sparse Core Ops, SparseCore 0:
  15.0 104.1 all-gather.1
where the time goes:
time: 298 us; the launch traced here: 297 us
  waiting for transfers between devices  113 us (38%)
  matrix products  66.5 us (22%)
  local copies, waits for them, and re-layouts  63.2 us (21%)
  other arithmetic  39.1 us (13%)
  between operations  13.6 us (5%)
    all_gather x1, waiting for transfers between devices, per_device(): collected_rows = lax.all_gather(stacked, 'ctx', axis=0, tiled=True)  100 us
    dot_general x4, matrix products, per_device(): jnp.einsum('hgqk,khd->hgqd', weights, every_value_row[:, key_value_head:k...  32.2 us
    reduce_sum x4, other arithmetic, per_device(): total = jnp.sum(expo, axis=-1)  31.9 us
    dot_general x4, matrix products, per_device(): jnp.einsum('qhgd,khd->hgqk', query_head_count[:, key_value_head:key_value...  29.2 us
    slice x1, local copies, waits for them, and re-layouts, per_device(): key_part = every_key_row[:, key_value_head:key_value_head + 1]  26.4 us
    ppermute x1, waiting for transfers between devices, from_behind(): return lax.ppermute(block, axis, route)  13.3 us
    reshape x1, local copies, waits for them, and re-layouts, per_device(): collected_rows[:, :key_value_width]  12.5 us
    slice x1, local copies, waits for them, and re-layouts, per_device(): collected_rows[:, key_value_width:]  11.3 us
  transfers between devices with their start and end apart: 2, of which 2 were waited for; matrix products, arithmetic and copies ran while one was open for 1% of the time, Pallas kernels for 0%

commit v1 on v0

--- a/solution.py
+++ b/solution.py
@@ -60,7 +60,9 @@
     own_docs = lax.dynamic_slice_in_dim(sequence_docs, first_row, count_of_rows, 0)
     score_scale = 1.0 / math.sqrt(HEAD_SIZE)
     stacked = jnp.concatenate([key_matrix, value_matrix], axis=1)
-    collected_rows = lax.all_gather(stacked, "ctx", axis=0, tiled=True)
+    collected_rows = jnp.concatenate(
+        lax.all_to_all(jnp.stack([stacked] * lax.axis_size("ctx")), "ctx", 0, 0), axis=0
+    )
     sequence_length = collected_rows.shape[0]
     every_key_row = collected_rows[:, :key_value_width].reshape(
         sequence_length, KEY_VALUE_HEADS, HEAD_SIZE

time: 298 us -> 520 us (1.74)
  the two profiles are of different devices: /device:TPU:1 before, /device:TPU:48 now
where the time goes in v1:
time: 520 us; the launch traced here: 519 us
  waiting for transfers between devices  382 us (73%)
  matrix products  65.2 us (13%)
  other arithmetic  38.1 us (7%)
  local copies, waits for them, and re-layouts  20.8 us (4%)
  starting transfers between devices  13.4 us (3%)
    all_to_all x1, waiting for transfers between devices, per_device(): lax.all_to_all(jnp.stack([stacked] * lax.axis_size('ctx')), 'ctx', 0, 0)  368 us
    dot_general x4, matrix products, per_device(): jnp.einsum('hgqk,khd->hgqd', weights, every_value_row[:, key_value_head:k...  32.1 us
    reduce_sum x4, other arithmetic, per_device(): total = jnp.sum(expo, axis=-1)  31.9 us
    dot_general x4, matrix products, per_device(): jnp.einsum('qhgd,khd->hgqk', query_head_count[:, key_value_head:key_value...  28.1 us
    ppermute x1, waiting for transfers between devices, from_behind(): return lax.ppermute(block, axis, route)  13.5 us
    all_to_all x1, starting transfers between devices, per_device(): lax.all_to_all(jnp.stack([stacked] * lax.axis_size('ctx')), 'ctx', 0, 0)  11.9 us
  transfers between devices with their start and end apart: 2, of which 2 were waited for; matrix products, arithmetic and copies ran while one was open for 1% of the time, Pallas kernels for 0%

profile of v1, /device:TPU:48, one launch (start us, length us, event | category | flops | bytes accessed | tf_op | source)
XLA Modules:
  0.0 519.4 jit_solution(15517045514077093117)
XLA Ops:
  0.0 1.5 fusion.27
  1.5 5.0 fusion.20
  6.6 0.1 reshape.298
  6.7 0.3 multiply_cosine_fusion
  7.0 0.3 subtract_convert_fusion
  7.3 0.2 pad_maximum_fusion.2
  7.6 0.2 copy.27
  7.8 6.2 %stack.2 = bf16[64,128,1024]{1,2,0:T(8,128)(2,1)} broadcast(bf16[128,1024]{0,1:T(8,128)(2,1)S(1)} %copy.27), dimensions={1,2} | broadcast | bytes 17039360 | tf_op jit(solution)/shard_map/stack | solution.py:64
  14.0 0.0 copy-start
  14.0 0.0 copy-start.1
  14.0 0.0 copy-start.2
  14.0 11.9 %all-to-all-start = ((bf16[64,128,1024]{1,2,0:T(8,128)(2,1)}), bf16[64,128,1024]{1,2,0:T(8,128)(2,1)}, u32[]{:S(2)}, u32[]{:S(2)}) async-start(bf16[64,128,1024]{1,2,0:T(8,128)(2,1)} %stack.2), calls=%async_computation | async-start | bytes 33554432 | tf_op jit(solution)/shard_map/all_to_all | solution.py:64
  25.9 0.0 copy-done
  25.9 0.3 copy.30
  26.2 0.0 copy-done.1
  26.2 0.0 copy-done.2
  26.2 3.7 fusion.26
  29.9 368.1 %all-to-all-done = bf16[64,128,1024]{1,2,0:T(8,128)(2,1)} async-done(((bf16[64,128,1024]{1,2,0:T(8,128)(2,1)}), bf16[64,128,1024]{1,2,0:T(8,128)(2,1)}, u32[]{:S(2)}, u32[]{:S(2)}) %all-to-all-start) | async-done | bytes 16777248 | tf_op jit(solution)/shard_map/all_to_all | solution.py:64
  398.0 8.7 %copy_bitcast_fusion = bf16[8192,1024]{0,1:T(8,128)(2,1)S(1)} fusion(bf16[64,128,1024]{1,2,0:T(8,128)(2,1)} %all-to-all-done), kind=kLoop, calls=%fused_computation | loop fusion | bytes 33554432 | tf_op jit(solution)/shard_map/reshape | solution.py:63
  406.7 4.2 fusion.57
  410.9 7.0 %fusion.61 = (f32[4,128]{1,0:T(4,128)S(1)}, f32[1,4,128,8192]{2,3,1,0:T(8,128)}) fusion(bf16[128,4,4,128]{0,3,2,1:T(8,128)(2,1)S(1)} %bitcast.172, bf16[8192,4,128]{0,2,1:T(8,128)(2,1)S(1)} %bitcast.166, pred[128,8192]{0,1:T(8,128)(4,1)S(1)} %fusion.26), kind=kOutput, calls=%fused_computation.79 | convolution fusion | flops 1086324224 | bytes 20056064 | tf_op jit(solution)/shard_map/qhgd,khd->hgqk/dot_general | solution.py:78
  417.9 7.0 %fusion.60 = (f32[4,128]{1,0:T(4,128)S(1)}, f32[1,4,128,8192]{2,3,1,0:T(8,128)}) fusion(bf16[128,4,4,128]{0,3,2,1:T(8,128)(2,1)S(1)} %bitcast.173, bf16[8192,4,128]{0,2,1:T(8,128)(2,1)S(1)} %bitcast.167, pred[128,8192]{0,1:T(8,128)(4,1)S(1)} %fusion.26), kind=kOutput, calls=%fused_computation.78 | convolution fusion | flops 1086324224 | bytes 20056064 | tf_op jit(solution)/shard_map/qhgd,khd->hgqk/dot_general | solution.py:78
  424.9 7.0 %fusion.59 = (f32[4,128]{1,0:T(4,128)S(1)}, f32[1,4,128,8192]{2,3,1,0:T(8,128)}) fusion(bf16[128,4,4,128]{0,3,2,1:T(8,128)(2,1)S(1)} %bitcast.174, bf16[8192,4,128]{0,2,1:T(8,128)(2,1)S(1)} %bitcast.168, pred[128,8192]{0,1:T(8,128)(4,1)S(1)} %fusion.26), kind=kOutput, calls=%fused_computation.77 | convolution fusion | flops 1086324224 | bytes 20056064 | tf_op jit(solution)/shard_map/qhgd,khd->hgqk/dot_general | solution.py:78
  432.0 7.0 %fusion.58 = (f32[4,128]{1,0:T(4,128)S(1)}, f32[1,4,128,8192]{2,3,1,0:T(8,128)}) fusion(bf16[128,4,4,128]{0,3,2,1:T(8,128)(2,1)S(1)} %bitcast.175, bf16[8192,4,128]{0,2,1:T(8,128)(2,1)S(1)} %bitcast.169, pred[128,8192]{0,1:T(8,128)(4,1)S(1)} %fusion.26), kind=kOutput, calls=%fused_computation.76 | convolution fusion | flops 1086324224 | bytes 20056064 | tf_op jit(solution)/shard_map/qhgd,khd->hgqk/dot_general | solution.py:78
  439.0 7.9 %fusion = f32[4,128]{1,0:T(4,128)S(1)} fusion(f32[1,4,128,8192]{2,3,1,0:T(8,128)} %get-tuple-element.18, f32[4,128]{1,0:T(4,128)S(1)} %get-tuple-element.17), kind=kLoop, calls=%fused_computation.9 | loop fusion | flops 8388096 | bytes 16781312 | tf_op jit(solution)/shard_map/reduce_sum | solution.py:93
  447.0 8.2 %fusion.32 = f32[1,4,128,128]{2,3,1,0:T(8,128)S(1)} fusion(f32[1,4,128,8192]{2,3,1,0:T(8,128)} %get-tuple-element.18, f32[4,128]{1,0:T(4,128)S(1)} %get-tuple-element.17, bf16[8192,4,128]{0,2,1:T(8,128)(2,1)} %bitcast.162, f32[4,128]{1,0:T(4,128)S(1)} %fusion), kind=kOutput, calls=%fused_computation.46 | convolution fusion | flops 1082195968 | bytes 19140608 | tf_op jit(solution)/shard_map/hgqk,khd->hgqd/dot_general | solution.py:95
  455.1 8.0 %fusion.2 = f32[4,128]{1,0:T(4,128)S(1)} fusion(f32[1,4,128,8192]{2,3,1,0:T(8,128)} %get-tuple-element.16, f32[4,128]{1,0:T(4,128)S(1)} %get-tuple-element.15), kind=kLoop, calls=%fused_computation.11 | loop fusion | flops 8388096 | bytes 16781312 | tf_op jit(solution)/shard_map/reduce_sum | solution.py:93
  463.1 8.0 %fusion.38 = f32[1,4,128,128]{2,3,1,0:T(8,128)S(1)} fusion(f32[1,4,128,8192]{2,3,1,0:T(8,128)} %get-tuple-element.16, f32[4,128]{1,0:T(4,128)S(1)} %get-tuple-element.15, bf16[8192,4,128]{0,2,1:T(8,128)(2,1)} %bitcast.163, f32[4,128]{1,0:T(4,128)S(1)} %fusion.2), kind=kOutput, calls=%fused_computation.48 | convolution fusion | flops 1082195968 | bytes 19140608 | tf_op jit(solution)/shard_map/hgqk,khd->hgqd/dot_general | solution.py:95
  471.1 8.0 %fusion.4 = f32[4,128]{1,0:T(4,128)S(1)} fusion(f32[1,4,128,8192]{2,3,1,0:T(8,128)} %get-tuple-element.14, f32[4,128]{1,0:T(4,128)S(1)} %get-tuple-element.13), kind=kLoop, calls=%fused_computation.13 | loop fusion | flops 8388096 | bytes 16781312 | tf_op jit(solution)/shard_map/reduce_sum | solution.py:93
  479.1 8.0 %fusion.44 = f32[1,4,128,128]{2,3,1,0:T(8,128)S(1)} fusion(f32[1,4,128,8192]{2,3,1,0:T(8,128)} %get-tuple-element.14, f32[4,128]{1,0:T(4,128)S(1)} %get-tuple-element.13, bf16[8192,4,128]{0,2,1:T(8,128)(2,1)} %bitcast.164, f32[4,128]{1,0:T(4,128)S(1)} %fusion.4), kind=kOutput, calls=%fused_computation.50 | convolution fusion | flops 1082195968 | bytes 19140608 | tf_op jit(solution)/shard_map/hgqk,khd->hgqd/dot_general | solution.py:95
  487.0 8.0 %fusion.6 = f32[4,128]{1,0:T(4,128)S(1)} fusion(f32[1,4,128,8192]{2,3,1,0:T(8,128)} %get-tuple-element.12, f32[4,128]{1,0:T(4,128)S(1)} %get-tuple-element.11), kind=kLoop, calls=%fused_computation.15 | loop fusion | flops 8388096 | bytes 16781312 | tf_op jit(solution)/shard_map/reduce_sum | solution.py:93
  495.0 8.0 %fusion.50 = f32[1,4,128,128]{2,3,1,0:T(8,128)S(1)} fusion(f32[1,4,128,8192]{2,3,1,0:T(8,128)} %get-tuple-element.12, f32[4,128]{1,0:T(4,128)S(1)} %get-tuple-element.11, bf16[8192,4,128]{0,2,1:T(8,128)(2,1)} %bitcast.165, f32[4,128]{1,0:T(4,128)S(1)} %fusion.6), kind=kOutput, calls=%fused_computation.52 | convolution fusion | flops 1082195968 | bytes 19140608 | tf_op jit(solution)/shard_map/hgqk,khd->hgqd/dot_general | solution.py:95
  503.0 0.1 pad_maximum_fusion
  503.1 0.3 copy.42
  503.4 0.1 multiply_convert_fusion
  503.5 1.6 collective-permute-start
  505.1 13.5 %collective-permute-done = bf16[1,128,2048]{2,1,0:T(8,128)(2,1)S(1)} collective-permute-done((bf16[1,128,2048]{2,1,0:T(8,128)(2,1)S(1)}, bf16[1,128,2048]{2,1,0:T(8,128)(2,1)S(1)}, u32[]{:S(2)}, u32[]{:S(2)}) %collective-permute-start) | collective-permute-done | bytes 524320 | tf_op jit(solution)/shard_map/ppermute | solution.py:16
  518.6 0.8 copy.61
  (9 shorter events, 0.1 us)
Async XLA Ops:
  14.0 11.9 %copy-start = (bf16[1,128,2048]{2,1,0:T(8,128)(2,1)S(1)}, bf16[1,128,2048]{2,1,0:T(8,128)(2,1)}, u32[]{:S(2)}) copy-start(bf16[1,128,2048]{2,1,0:T(8,128)(2,1)} %param.6) | copy-start | bytes 1572868
  14.0 12.2 %copy-start.1 = (s32[1,8192]{1,0:T(1,128)S(1)}, s32[1,8192]{1,0:T(1,128)}, u32[]{:S(2)}) copy-start(s32[1,8192]{1,0:T(1,128)} %param.8) | copy-start | bytes 98308
  14.0 12.2 %copy-start.2 = (s32[1,128]{1,0:T(1,128)S(1)}, s32[1,128]{1,0:T(1,128)}, u32[]{:S(2)}) copy-start(s32[1,128]{1,0:T(1,128)} %param.9) | copy-start | bytes 1540
  14.0 384.0 %all-to-all-start = ((bf16[64,128,1024]{1,2,0:T(8,128)(2,1)}), bf16[64,128,1024]{1,2,0:T(8,128)(2,1)}, u32[]{:S(2)}, u32[]{:S(2)}) async-start(bf16[64,128,1024]{1,2,0:T(8,128)(2,1)} %stack.2), calls=%async_computation | async-start | bytes 33554432 | tf_op jit(solution)/shard_map/all_to_all | solution.py:64
  503.5 15.1 %collective-permute-start = (bf16[1,128,2048]{2,1,0:T(8,128)(2,1)S(1)}, bf16[1,128,2048]{2,1,0:T(8,128)(2,1)S(1)}, u32[]{:S(2)}, u32[]{:S(2)}) collective-permute-start(bf16[1,128,2048]{2,1,0:T(8,128)(2,1)S(1)} %multiply_convert_fusion), channel_id=1, source_target_pairs={{192,0},{0,64},{64,128},{128,192},{193,1},{1,65},{65,129},{129,193... | collective-permute-start | bytes 1572872 | tf_op jit(solution)/shard_map/ppermute | solution.py:16
